TPU v7x, 768 devices: a whole 4x8x12 slice. The times are simulated.
768 devices in a mesh: rows: 384 (over z, x, y), cols: 2 (over core).
Axes of the slice: x: 4, y: 8, z: 12, core: 2. Of those that a mesh axis runs over, the one named last changes fastest.
Arguments:
- start: float32 [147456, 256], P('rows', 'cols'), may hold values from -24 to 24
- tiles: bfloat16 [13824, 128, 128], P('rows'), may hold values from -0.078125 to 0.078125
- tile_cols: int32 [13824], P('rows'), may hold values from 0 to 1151, as said below
Outputs:
- embedding: float32 [147456, 256], P('rows', 'cols')
Inputs may be any that keep to these rules, and one draw needn't show every extreme that they name: `tile_cols`: a tile of a block row held by rows index d has its column block from d * 3 - 2 to (d + 1) * 3 + 1.
All inputs are finite; a program needn't handle non-finite values.
Results may differ from a plain program's by a relative error of at most 0.007.
Values may be sent and summed in bfloat16 or wider, within the bound.
A program may use at most 32 MiB of HBM per device.

v0:
```python
import jax
import jax.numpy as jnp
from jax import lax
from jax.sharding import PartitionSpec as P

TILE = 128
TPR = 12
CUT = 2
DEGREE = 3
ITERS = 2


def extended_2(block, sides, width):
    for axis, dim in sides:
        count = lax.axis_size(axis)
        forward = [(i, i + 1) for i in range(count - 1)]
        backward = [(target, source) for source, target in forward]
        low = lax.ppermute(
            lax.slice_in_dim(block, block.shape[dim] - width, None, axis=dim), axis, forward
        )
        high = lax.ppermute(lax.slice_in_dim(block, 0, width, axis=dim), axis, backward)
        block = jnp.concatenate([low, block, high], axis=dim)
    return block


def apply_local(zmat, tiles, tile_cols):
    width = zmat.shape[1]
    block_rows = zmat.shape[0] // TILE
    extended = extended_2(zmat, (("rows", 0),), CUT * TILE)
    ext_blocks = extended.reshape(block_rows + 2 * CUT, TILE, width)
    lowest = lax.axis_index("rows") * block_rows - CUT
    local_cols = tile_cols - lowest
    selected = jnp.take(ext_blocks, local_cols, axis=0)
    product = jnp.einsum(
        "rtij,rtjc->ric",
        tiles.reshape(block_rows, TPR, TILE, TILE),
        selected.reshape(block_rows, TPR, TILE, width),
        preferred_element_type=jnp.float32,
    )
    return product.reshape(block_rows * TILE, width)


def per_device(start, tiles, tile_cols):
    current = start
    half = start.shape[1]
    node_count = start.shape[0] * lax.axis_size("rows")
    for outer in range(ITERS):
        y_prev = current
        product = apply_local(current.astype(jnp.bfloat16), tiles, tile_cols)
        y_curr = ((1.0 - 1.25) * current - product) / 0.75
        for step in range(1, DEGREE):
            product = apply_local(y_curr.astype(jnp.bfloat16), tiles, tile_cols)
            y_next = 2.0 * ((1.0 - 1.25) * y_curr - product) / 0.75 - y_prev
            y_prev = y_curr
            y_curr = y_next
        full_panel = lax.all_gather(y_curr, "cols", axis=1, tiled=True)
        partial_gram = jnp.dot(
            full_panel.T,
            full_panel,
            precision=lax.Precision.HIGHEST,
            preferred_element_type=jnp.float32,
        )
        gram = lax.psum(partial_gram, "rows") / node_count
        factor = jnp.linalg.cholesky(gram)
        inverse = lax.linalg.triangular_solve(
            factor, jnp.eye(gram.shape[0], dtype=gram.dtype), left_side=True, lower=True
        )
        own_rows = lax.dynamic_slice_in_dim(inverse, lax.axis_index("cols") * half, half, 0)
        current = jnp.dot(
            full_panel,
            own_rows.T,
            precision=lax.Precision.HIGHEST,
            preferred_element_type=jnp.float32,
        )
    return current


def solution(mesh):
    placed = (P("rows", "cols"), P("rows", None, None), P("rows"))
    return jax.shard_map(
        per_device, mesh=mesh, in_specs=placed, out_specs=P("rows", "cols"), check_vma=False
    )
```

profile of v0, /device:TPU:1, one launch (start us, length us, event | category | flops | bytes accessed | tf_op | source)
XLA Modules:
  0.0 989.5 jit_solution(3426880937057170345)
XLA Ops:
  7.6 4.0 collective-permute-start
  18.6 3.2 collective-permute-start.2
  23.2 4.6 collective-permute-done.3
  29.3 4.6 collective-permute-start.4
  35.2 4.0 collective-permute-done.5
  40.7 7.5 all_gather.6
  50.1 384.0 %all-reduce.4.cloned.1.call-done = f32[256,256]{0,1:T(8,128)} async-done(((f32[256,256]{0,1:T(8,128)}), f32[256,256]{0,1:T(8,128)}) %all-reduce.4.cloned.1.call-update) | async-done | bytes 262160 | tf_op jit(solution)/shard_map/psum | solution.py:63
  435.4 11.7 %cholesky.130 = f32[128,128]{1,0:T(8,128)S(1)} custom-call(f32[128,128]{1,0:T(8,128)S(1)} %cholesky.194), custom_call_target="Cholesky" | custom-call | tf_op jit(solution)/shard_map/jit(cholesky)/cholesky | solution.py:64
  447.2 9.8 custom-call.13
  457.5 11.7 %cholesky.147 = f32[128,128]{1,0:T(8,128)S(1)} custom-call(f32[128,128]{1,0:T(8,128)S(1)} %convolution_subtract_fusion.3), custom_call_target="Cholesky" | custom-call | tf_op jit(solution)/shard_map/jit(cholesky)/cholesky | solution.py:64
  471.3 4.3 while.4
  475.6 19.7 %custom-call.14 = f32[2,128,128]{1,2,0:T(8,128)S(1)} custom-call(f32[2,128,128]{2,1,0:T(8,128)S(1)} %get-tuple-element.22), custom_call_target="InvertDiagBlocksLowerTriangular" | custom-call | tf_op jit(solution)/shard_map/triangular_solve/custom-call.0 | solution.py:65
  500.0 3.8 collective-permute-done.7
  505.3 4.0 collective-permute-start.8
  510.7 3.8 collective-permute-done.9
  516.0 4.6 collective-permute-start.10
  521.9 3.7 collective-permute-done.11
  527.2 14.0 %all_gather.7 = f32[384,256]{1,0:T(8,128)S(1)} all-gather(f32[384,128]{1,0:T(8,128)S(1)} %fusion.4), channel_id=1, replica_groups=mesh['rows'=384,'cols'=2] {'cols'}, dimensions={1}, use_global_device_ids=true | all-gather | bytes 589824 | tf_op jit(solution)/shard_map/all_gather | solution.py:56
  542.8 375.9 %all-reduce.6.cloned.1.call-done = f32[256,256]{0,1:T(8,128)} async-done(((f32[256,256]{0,1:T(8,128)}), f32[256,256]{0,1:T(8,128)}) %all-reduce.6.cloned.1.call-update) | async-done | bytes 262160 | tf_op jit(solution)/shard_map/psum | solution.py:63
  920.0 11.7 %cholesky.164 = f32[128,128]{1,0:T(8,128)S(1)} custom-call(f32[128,128]{1,0:T(8,128)S(1)} %cholesky.197), custom_call_target="Cholesky" | custom-call | tf_op jit(solution)/shard_map/jit(cholesky)/cholesky | solution.py:64
  931.7 9.8 custom-call.15
  942.0 11.7 %cholesky.181 = f32[128,128]{1,0:T(8,128)S(1)} custom-call(f32[128,128]{1,0:T(8,128)S(1)} %convolution_subtract_fusion.2), custom_call_target="Cholesky" | custom-call | tf_op jit(solution)/shard_map/jit(cholesky)/cholesky | solution.py:64
  956.5 4.2 while.5
  960.7 19.7 %custom-call.16 = f32[2,128,128]{1,2,0:T(8,128)S(1)} custom-call(f32[2,128,128]{2,1,0:T(8,128)S(1)} %get-tuple-element.23), custom_call_target="InvertDiagBlocksLowerTriangular" | custom-call | tf_op jit(solution)/shard_map/triangular_solve/custom-call.0 | solution.py:65
  (115 shorter events, 44.6 us)
Async XLA Ops:
  6.5 11.1 %copy-start = (bf16[36,128,128]{2,1,0:T(8,128)(2,1)S(1)}, bf16[36,128,128]{2,1,0:T(8,128)(2,1)}, u32[]{:S(2)}) copy-start(bf16[36,128,128]{2,1,0:T(8,128)(2,1)} %param.9) | copy-start | bytes 3538948
  6.5 427.6 %all-reduce.4.cloned.1.call-start = ((), (), s32[]{:S(2)}) async-start(), calls=%async_computation | async-start | bytes 524288 | tf_op jit(solution)/shard_map/psum | solution.py:63
  7.6 6.0 collective-permute-start
  11.6 5.0 collective-permute-start.1
  17.6 0.9 copy-start.1
  18.6 4.5 collective-permute-start.2
  21.8 5.9 collective-permute-start.3
  29.3 5.9 collective-permute-start.4
  33.9 5.3 collective-permute-start.5
  49.8 868.9 %all-reduce.6.cloned.1.call-start = ((), (), s32[]{:S(2)}) async-start(), calls=%async_computation.1 | async-start | bytes 524288 | tf_op jit(solution)/shard_map/psum | solution.py:63
  434.1 1.2 copy-start.2
  496.8 3.2 collective-permute-start.6
  498.6 5.2 collective-permute-start.7
  505.3 5.4 collective-permute-start.8
  509.4 5.1 collective-permute-start.9
  516.0 5.9 collective-permute-start.10
  520.6 5.0 collective-permute-start.11
  918.7 1.2 copy-start.3
Sparse Core Ops, SparseCore 0:
  49.9 384.1 all-reduce.3
  542.9 375.7 all-reduce.5
where the time goes:
time: 999 us; the launch traced here: 989 us
  waiting for transfers between devices  783 us (78%)
  other arithmetic  113 us (11%)
  starting transfers between devices  30.3 us (3%)
  blocking collectives  21.5 us (2%)
  between operations  16.8 us (2%)
  local copies, waits for them, and re-layouts  13.6 us (1%)
  matrix products  10.3 us (1%)
    psum x2, waiting for transfers between devices, per_device(): gram = lax.psum(partial_gram, 'rows') / node_count  760 us
    another operation x13, other arithmetic, per_device(): factor = jnp.linalg.cholesky(gram)  68.7 us
    another operation x5, other arithmetic, per_device(): lax.linalg.triangular_solve(factor, jnp.eye(gram.shape[0], dtype=gram.dty...  39.4 us
    ppermute x6, waiting for transfers between devices, extended_2(): lax.ppermute(lax.slice_in_dim(block, 0, width, axis=dim), axis, backward)  23 us
    ppermute x6, starting transfers between devices, extended_2(): lax.ppermute(lax.slice_in_dim(block, block.shape[dim] - width, None, axis...  22.3 us
    all_gather x2, blocking collectives, per_device(): full_panel = lax.all_gather(y_curr, 'cols', axis=1, tiled=True)  21.5 us
  transfers between devices with their start and end apart: 14, of which 8 were waited for; matrix products, arithmetic and copies ran while one was open for 0% of the time, Pallas kernels for 0%

commit v1 on v0

v1 whole, which is shorter than its diff:
```python
import functools

import jax
import jax.numpy as jnp
from jax import lax
from jax.experimental import pallas as pl
from jax.experimental.pallas import tpu as pltpu
from jax.sharding import PartitionSpec as P

TILE = 128
BR = 3
TPR = 12
CUT = 2
SPAN = BR + 2 * CUT
DEGREE = 3
ITERS = 2
OWN = BR * TILE
EXT = SPAN * TILE
LOW = CUT * TILE
AXES = (12, 4, 8)
MESH = pl.DeviceIdType.MESH
VMEM = pl.BlockSpec(memory_space=pltpu.VMEM)
F32 = jnp.float32
BF16 = jnp.bfloat16
HIGHEST = lax.Precision.HIGHEST


def dot(a, b, contract, precision=None):
    return lax.dot_general(
        a, b, (contract, ((), ())), precision=precision, preferred_element_type=F32
    )


def band_kernel(cols_ref, tiles_ref, band_ref):
    lowest = lax.axis_index("rows") * BR - CUT
    for r in range(BR):
        sums = [jnp.zeros((TILE, TILE), F32) for _ in range(SPAN)]
        for t in range(TPR):
            tile = tiles_ref[r * TPR + t].astype(F32)
            place = cols_ref[r * TPR + t] - lowest
            for b in range(SPAN):
                sums[b] = sums[b] + jnp.where(place == b, tile, 0.0)
        for b in range(SPAN):
            high = sums[b].astype(BF16)
            rows = slice(r * TILE, (r + 1) * TILE)
            lanes = slice(b * TILE, (b + 1) * TILE)
            band_ref[0, rows, lanes] = high
            band_ref[1, rows, lanes] = (sums[b] - high.astype(F32)).astype(BF16)


def build_band(tiles, tile_cols):
    return pl.pallas_call(
        band_kernel,
        out_shape=jax.ShapeDtypeStruct((2, OWN, EXT), BF16),
        in_specs=[pl.BlockSpec(memory_space=pltpu.SMEM), VMEM],
        out_specs=VMEM,
        name="band",
    )(tile_cols, tiles)


def filter_kernel(
    axes, x_ref, band_ref, full_ref, gram_ref,
    z, y1, part, rx, s1, ry, rz,
    halo_s, halo_r, pair_s, pair_r, x_s, x_r, y_s, y_r, z_s, z_r, gy_s, gy_r, gx_s, gx_r, gc_s, gc_r,
):
    NZ, NX, NY = axes
    T = 32 // (NX * NY)
    me = lax.axis_index("rows")
    core = lax.axis_index("cols")
    my_z, my_x, my_y = me // (NX * NY), (me // NY) % NX, me % NY
    count = NZ * NX * NY

    def row(zz, xx, yy):
        return (zz * NX + xx) * NY + yy

    right, left = lax.rem(me + 1, count), lax.rem(me + count - 1, count)
    to_x = [row(my_z, lax.rem(my_x + d, NX), my_y) for d in range(NX)]
    to_y = [row(my_z, my_x, lax.rem(my_y + d, NY)) for d in range(NY)]
    to_z = [row(lax.rem(my_z + d, NZ), my_x, my_y) for d in range(NZ)]

    barrier = pltpu.get_barrier_semaphore()
    greet = [(left, core), (right, core), (me, 1 - core)]
    greet += [(r, core) for r in to_x[1:] + to_y[1:] + to_z[1:]]
    greet += [(r, 1 - core) for r in to_x[1:]]
    for device in greet:
        pl.semaphore_signal(barrier, inc=1, device_id=device, device_id_type=MESH)
    pl.semaphore_wait(barrier, len(greet))

    def remote(src, dst, send, recv, device):
        return pltpu.make_async_remote_copy(
            src_ref=src, dst_ref=dst, send_sem=send, recv_sem=recv,
            device_id=device, device_id_type=MESH,
        )

    sent = []

    def start(copy):
        copy.start()
        sent.append(copy)

    def band_dot(lanes, values):
        return dot(band_ref[0, :, lanes], values, ((1,), (0,))) + dot(
            band_ref[1, :, lanes], values, ((1,), (0,))
        )

    own = slice(LOW, LOW + OWN)
    y_prev = None
    for step in range(DEGREE):
        current = x_ref if step == 0 else y1 if step == 1 else part
        y_curr = current[...]
        z[step, own, :] = y_curr.astype(BF16)
        down = remote(
            z.at[step, pl.ds(LOW, LOW)], z.at[step, pl.ds(LOW + OWN, LOW)],
            halo_s.at[step, 0], halo_r.at[step, 0], (left, core),
        )
        up = remote(
            z.at[step, pl.ds(OWN, LOW)], z.at[step, pl.ds(0, LOW)],
            halo_s.at[step, 1], halo_r.at[step, 1], (right, core),
        )
        start(down)
        start(up)
        product = band_dot(own, z[step, own, :])
        up.wait_recv()
        product += band_dot(slice(0, LOW), z[step, 0:LOW, :])
        down.wait_recv()
        product += band_dot(slice(LOW + OWN, EXT), z[step, LOW + OWN : EXT, :])
        if step == 0:
            y1[...] = ((1.0 - 1.25) * y_curr - product) / 0.75
        elif step == 1:
            part[...] = 2.0 * ((1.0 - 1.25) * y_curr - product) / 0.75 - x_ref[...]
        else:
            full_ref[core] = 2.0 * ((1.0 - 1.25) * y_curr - product) / 0.75 - y1[...]

    pair = remote(full_ref.at[core], full_ref.at[core], pair_s, pair_r, (me, 1 - core))
    start(pair)
    pair.wait_recv()
    mine = full_ref[core]
    local = s1
    for half in range(2):
        block = dot(full_ref[half], mine, ((0,), (0,)), HIGHEST)
        for t in range(16):
            tile = half * 16 + t
            k, xx, yy = tile % T, tile // T % NX, tile // (T * NX)
            local[xx, yy, k] = block[8 * t : 8 * t + 8, :]

    for d in range(1, NX):
        start(remote(local.at[lax.rem(my_x + d, NX)], rx.at[d], x_s.at[d], x_r.at[d], (to_x[d], core)))
    rx[0] = local[my_x]
    for d in range(1, NX):
        remote(local.at[0], rx.at[d], x_s.at[d], x_r.at[d], (to_x[d], core)).wait_recv()
    total = rx[0]
    for d in range(1, NX):
        total += rx[d]
    rx[0] = total
    for d in range(1, NY):
        start(remote(rx.at[0, lax.rem(my_y + d, NY)], ry.at[d], y_s.at[d], y_r.at[d], (to_y[d], core)))
    ry[0] = rx[0, my_y]
    for d in range(1, NY):
        remote(rx.at[0, 0], ry.at[d], y_s.at[d], y_r.at[d], (to_y[d], core)).wait_recv()
    total = ry[0]
    for d in range(1, NY):
        total += ry[d]
    rz[my_z] = total
    for d in range(1, NZ):
        start(remote(rz.at[my_z], rz.at[my_z], z_s.at[d], z_r.at[d], (to_z[d], core)))
    for d in range(1, NZ):
        remote(rz.at[0], rz.at[0], z_s.at[d], z_r.at[d], (to_z[d], core)).wait_recv()
    total = rz[0]
    for d in range(1, NZ):
        total += rz[d]
    gram_ref[core, my_x, my_y] = total / (count * OWN)
    for d in range(1, NY):
        chunk = gram_ref.at[core, my_x, my_y]
        start(remote(chunk, chunk, gy_s.at[d], gy_r.at[d], (to_y[d], core)))
    for d in range(1, NY):
        chunk = gram_ref.at[0, 0, 0]
        remote(chunk, chunk, gy_s.at[d], gy_r.at[d], (to_y[d], core)).wait_recv()
    slab = gram_ref.at[core, my_x]
    for d in range(1, NX):
        start(remote(slab, slab, gx_s.at[d], gx_r.at[d], (to_x[d], core)))

    def cross(d):
        return remote(slab, slab, gc_s.at[d], gc_r.at[d], (to_x[d], 1))

    @pl.when(core == 0)
    def _():
        for d in range(NX):
            cross(d).start()

    for d in range(1, NX):
        remote(slab, slab, gx_s.at[d], gx_r.at[d], (to_x[d], core)).wait_recv()

    @pl.when(core == 1)
    def _():
        for d in range(NX):
            remote(slab, slab, gc_s.at[d], gc_r.at[d], (me, 0)).wait_recv()

    @pl.when(core == 0)
    def _():
        for d in range(NX):
            cross(d).wait_send()

    for copy in sent:
        copy.wait_send()


def filter_and_gram(axes, x, band):
    NZ, NX, NY = axes
    T = 32 // (NX * NY)
    dma = pltpu.SemaphoreType.DMA
    return pl.pallas_call(
        functools.partial(filter_kernel, axes),
        out_shape=(
            jax.ShapeDtypeStruct((2, OWN, TILE), F32),
            jax.ShapeDtypeStruct((2, NX, NY, T, 8, TILE), F32),
        ),
        in_specs=[VMEM, VMEM],
        out_specs=(VMEM, VMEM),
        scratch_shapes=[
            pltpu.VMEM((DEGREE, EXT, TILE), BF16),
            pltpu.VMEM((OWN, TILE), F32),
            pltpu.VMEM((OWN, TILE), F32),
            pltpu.VMEM((NX, NY, T, 8, TILE), F32),
            pltpu.VMEM((NX, NY, T, 8, TILE), F32),
            pltpu.VMEM((NY, T, 8, TILE), F32),
            pltpu.VMEM((NZ, T, 8, TILE), F32),
            dma((DEGREE, 2)), dma((DEGREE, 2)), dma, dma,
            dma((NX,)), dma((NX,)), dma((NY,)), dma((NY,)), dma((NZ,)), dma((NZ,)),
            dma((NY,)), dma((NY,)), dma((NX,)), dma((NX,)), dma((NX,)), dma((NX,)),
        ],
        compiler_params=pltpu.CompilerParams(collective_id=0, has_side_effects=True),
        name="filter",
    )(x, band)


def lane_copy(v, c):
    return jnp.broadcast_to(v[:, c : c + 1], (8, TILE))


def row_copy(v, r):
    return jnp.broadcast_to(v[r : r + 1, :], (8, TILE))


def inverse_factor(m):
    lane = lax.broadcasted_iota(jnp.int32, (8, TILE), 1)
    sub = lax.broadcasted_iota(jnp.int32, (8, TILE), 0)
    m = list(m)
    w = [None] * 16
    for g in range(16):
        first = 8 * g
        spread = [lane_copy(m[g], first + k) for k in range(8)]
        a = [[row_copy(spread[k], i) if i >= k else None for k in range(8)] for i in range(8)]
        inside = (lane >= first) & (lane < first + 8)
        rows = jnp.where(inside, jnp.where(lane == sub + first, 1.0, 0.0), m[g])
        r = [None] * 8
        c = [[None] * 8 for _ in range(8)]
        for k in range(8):
            r[k] = lax.rsqrt(a[k][k])
            for i in range(k + 1, 8):
                c[i][k] = a[i][k] * r[k]
            for j in range(k + 1, 8):
                for i in range(j, 8):
                    a[i][j] = a[i][j] - c[i][k] * c[j][k]
        solved = [row_copy(rows, k) for k in range(8)]
        for k in range(8):
            solved[k] = solved[k] * r[k]
            for j in range(k + 1, 8):
                solved[j] = solved[j] - c[j][k] * solved[k]
        group = solved[0]
        for k in range(1, 8):
            group = jnp.where(sub == k, solved[k], group)
        w[g] = jnp.where(lane < first + 8, group, 0.0)
        for i in range(g + 1, 16):
            p = [lane_copy(m[i], first + k) for k in range(8)]
            rest = jnp.where(inside, 0.0, m[i])
            for k in range(8):
                col = p[k] * r[k]
                for j in range(k + 1, 8):
                    p[j] = p[j] - c[j][k] * col
                rest = rest - col * solved[k]
            m[i] = rest
    return w


def update_kernel(axes, full_ref, gram_ref, out_ref, gaa, gba, gbb, waa, wbb):
    NZ, NX, NY = axes
    T = 32 // (NX * NY)
    core = lax.axis_index("cols")
    for t in range(16):
        for half, panel, dst in ((0, 0, gaa), (1, 0, gba), (1, 1, gbb)):
            tile = half * 16 + t
            k, xx, yy = tile % T, tile // T % NX, tile // (T * NX)
            dst[8 * t : 8 * t + 8, :] = gram_ref[panel, xx, yy, k]
    for t, group in enumerate(inverse_factor([gaa[8 * i : 8 * i + 8, :] for i in range(16)])):
        waa[8 * t : 8 * t + 8, :] = group

    @pl.when(core == 0)
    def _():
        out_ref[...] = dot(full_ref[0], waa[...], ((1,), (1,)), HIGHEST)

    @pl.when(core == 1)
    def _():
        cba = dot(gba[...], waa[...], ((1,), (1,)), HIGHEST)
        gbb[...] = gbb[...] - dot(cba, cba, ((1,), (1,)), HIGHEST)
        shift = dot(cba, waa[...], ((1,), (0,)), HIGHEST)
        rest = full_ref[1] - dot(full_ref[0], shift, ((1,), (1,)), HIGHEST)
        for t, group in enumerate(inverse_factor([gbb[8 * i : 8 * i + 8, :] for i in range(16)])):
            wbb[8 * t : 8 * t + 8, :] = group
        out_ref[...] = dot(rest, wbb[...], ((1,), (1,)), HIGHEST)


def orthogonalize(axes, full, gram):
    square = pltpu.VMEM((TILE, TILE), F32)
    return pl.pallas_call(
        functools.partial(update_kernel, axes),
        out_shape=jax.ShapeDtypeStruct((OWN, TILE), F32),
        in_specs=[VMEM, VMEM],
        out_specs=VMEM,
        scratch_shapes=[square] * 5,
        name="orthogonalize",
    )(full, gram)


def per_device(axes, start, tiles, tile_cols):
    band = build_band(tiles, tile_cols)
    x = start
    for _ in range(ITERS):
        full, gram = filter_and_gram(axes, x, band)
        x = orthogonalize(axes, full, gram)
    return x


def solution(mesh, axes=AXES):
    placed = (P("rows", "cols"), P("rows", None, None), P("rows"))
    return jax.shard_map(
        functools.partial(per_device, axes),
        mesh=mesh, in_specs=placed, out_specs=P("rows", "cols"), check_vma=False,
    )
```

time: 999 us -> 143 us (0.14)
  waiting for transfers between devices: 783 us -> 0 us
  Pallas kernels: 0 us -> 142 us
  other arithmetic: 113 us -> 0 us
  starting transfers between devices: 30.3 us -> 0 us
  blocking collectives: 21.5 us -> 0 us
  between operations: 16.8 us -> 0.02 us
  local copies, waits for them, and re-layouts: 13.6 us -> 0 us
  matrix products: 10.3 us -> 0 us
    psum x2 -> x0, waiting for transfers between devices: 760 us -> none  [per_device(): gram = lax.psum(partial_gram, 'rows') / node_count]
    pallas_call x0 -> x5, Pallas kernels: none -> 142 us  [the longest x2 116 us: filter_and_gram(): pl.pallas_call(functools.partial(filter_kernel, axes), out_shape=(jax.Sha...]
    another operation x18 -> x0, other arithmetic: 108 us -> none  [the longest x13 68.7 us: per_device(): factor = jnp.linalg.cholesky(gram)]
    ppermute x12 -> x0, starting transfers between devices: 30 us -> none  [the longest x6 22.3 us: extended_2(): lax.ppermute(lax.slice_in_dim(block, block.shape[dim] - width, None, axis...]
    ppermute x12 -> x0, waiting for transfers between devices: 23 us -> none  [the longest x6 23 us: extended_2(): lax.ppermute(lax.slice_in_dim(block, 0, width, axis=dim), axis, backward)]
    all_gather x2 -> x0, blocking collectives: 21.5 us -> none  [per_device(): full_panel = lax.all_gather(y_curr, 'cols', axis=1, tiled=True)]
  transfers between devices with their start and end apart: 14 -> 0, of which waited for: 8 -> 0; matrix products, arithmetic and copies ran while one was open for 0% -> 0% of each run, Pallas kernels for 0% -> 0%
where the time goes in v1:
time: 143 us; the launch traced here: 142 us
  Pallas kernels  142 us (99%)
    pallas_call x2, Pallas kernels, filter_and_gram(): pl.pallas_call(functools.partial(filter_kernel, axes), out_shape=(jax.Sha...  116 us
    pallas_call x2, Pallas kernels, orthogonalize(): pl.pallas_call(functools.partial(update_kernel, axes), out_shape=jax.Shap...  22.4 us
    pallas_call x1, Pallas kernels, build_band(): pl.pallas_call(band_kernel, out_shape=jax.ShapeDtypeStruct((2, OWN, EXT),...  3.75 us

profile of v1, /device:TPU:1, one launch (start us, length us, event | category | flops | bytes accessed | tf_op | source)
XLA Modules:
  0.0 142.4 jit_solution(4915498863197651853)
XLA Ops:
  0.0 3.8 %band.1.band_ref = bf16[2,384,896]{2,1,0:T(8,128)(2,1)} custom-call(s32[36]{0:T(128)} %cols_ref.1, bf16[36,128,128]{2,1,0:T(8,128)(2,1)} %tiles_ref.1), custom_call_target="tpu_custom_call" | custom-call | tf_op jit(solution)/shard_map/band/pallas_call | solution.py:52
  3.8 66.0 %filter.2 = (f32[2,384,128]{2,1,0:T(8,128)}, f32[2,4,8,1,8,128]{5,4,3,2,1,0:T(8,128)}) custom-call(f32[384,128]{1,0:T(8,128)} %x_ref.1, bf16[2,384,896]{2,1,0:T(8,128)(2,1)} %band.1.band_ref), custom_call_target="tpu_custom_call" | custom-call | tf_op jit(solution)/shard_map/filter/pallas_call | solution.py:211
  69.8 11.2 %orthogonalize.2.x_ref = f32[384,128]{1,0:T(8,128)} custom-call(f32[2,384,128]{2,1,0:T(8,128)} %get-tuple-element.9.full_ref, f32[2,4,8,1,8,128]{5,4,3,2,1,0:T(8,128)} %get-tuple-element.10.gram_ref), custom_call_target="tpu_custom_call" | custom-call | tf_op jit(solution)/shard_map/orthogonalize/pallas_call | solution.py:314
  81.0 50.1 %filter.3 = (f32[2,384,128]{2,1,0:T(8,128)}, f32[2,4,8,1,8,128]{5,4,3,2,1,0:T(8,128)}) custom-call(f32[384,128]{1,0:T(8,128)} %orthogonalize.2.x_ref, bf16[2,384,896]{2,1,0:T(8,128)(2,1)} %band.1.band_ref), custom_call_target="tpu_custom_call" | custom-call | tf_op jit(solution)/shard_map/filter/pallas_call | solution.py:211
  131.1 11.2 %orthogonalize.3 = f32[384,128]{1,0:T(8,128)} custom-call(f32[2,384,128]{2,1,0:T(8,128)} %get-tuple-element.11.full_ref, f32[2,4,8,1,8,128]{5,4,3,2,1,0:T(8,128)} %get-tuple-element.12.gram_ref), custom_call_target="tpu_custom_call" | custom-call | tf_op jit(solution)/shard_map/orthogonalize/pallas_call | solution.py:314

commit v2 on v0

v2 whole, which is shorter than its diff:
```python
import functools

import jax
import jax.numpy as jnp
from jax import lax
from jax.experimental import pallas as pl
from jax.experimental.pallas import tpu as pltpu
from jax.sharding import PartitionSpec as P

TILE = 128
BR = 3
TPR = 12
CUT = 2
SPAN = BR + 2 * CUT
DEGREE = 3
ITERS = 2
OWN = BR * TILE
EXT = SPAN * TILE
LOW = CUT * TILE
AXES = (12, 4, 8)
MESH = pl.DeviceIdType.MESH
ANY = pl.BlockSpec(memory_space=pl.ANY)
F32 = jnp.float32
BF16 = jnp.bfloat16
HIGHEST = lax.Precision.HIGHEST


def dot(a, b, contract, precision=None):
    return lax.dot_general(
        a, b, (contract, ((), ())), precision=precision, preferred_element_type=F32
    )


def lane_copy(v, c):
    return jnp.broadcast_to(v[:, c : c + 1], (8, TILE))


def row_copy(v, r):
    return jnp.broadcast_to(v[r : r + 1, :], (8, TILE))


def inverse_factor(m):
    lane = lax.broadcasted_iota(jnp.int32, (8, TILE), 1)
    sub = lax.broadcasted_iota(jnp.int32, (8, TILE), 0)
    m = list(m)
    w = [None] * 16
    for g in range(16):
        first = 8 * g
        spread = [lane_copy(m[g], first + k) for k in range(8)]
        a = [[row_copy(spread[k], i) if i >= k else None for k in range(8)] for i in range(8)]
        inside = (lane >= first) & (lane < first + 8)
        rows = jnp.where(inside, jnp.where(lane == sub + first, 1.0, 0.0), m[g])
        r = [None] * 8
        c = [[None] * 8 for _ in range(8)]
        for k in range(8):
            r[k] = lax.rsqrt(a[k][k])
            for i in range(k + 1, 8):
                c[i][k] = a[i][k] * r[k]
            for j in range(k + 1, 8):
                for i in range(j, 8):
                    a[i][j] = a[i][j] - c[i][k] * c[j][k]
        solved = [row_copy(rows, k) for k in range(8)]
        for k in range(8):
            solved[k] = solved[k] * r[k]
            for j in range(k + 1, 8):
                solved[j] = solved[j] - c[j][k] * solved[k]
        group = solved[0]
        for k in range(1, 8):
            group = jnp.where(sub == k, solved[k], group)
        w[g] = jnp.where(lane < first + 8, group, 0.0)
        for i in range(g + 1, 16):
            p = [lane_copy(m[i], first + k) for k in range(8)]
            rest = jnp.where(inside, 0.0, m[i])
            for k in range(8):
                col = p[k] * r[k]
                for j in range(k + 1, 8):
                    p[j] = p[j] - c[j][k] * col
                rest = rest - col * solved[k]
            m[i] = rest
    return w


def kernel(
    axes, cols_ref, x_ref, tiles_ref, out_ref,
    tiles, band, x, z, y1, y2, y3, other, m, w, waa,
    part_a, part_b, plane_a, plane_b, line_a, line_b, gram_a, gram_b,
    load, halo_s, halo_r, pair_s, pair_r, plane_s, plane_r, line_s, line_r, gram_s, gram_r,
):
    NZ, NX, NY = axes
    NQ = NX * NY
    me = lax.axis_index("rows")
    core = lax.axis_index("cols")
    my_z, my_q = me // NQ, me % NQ
    my_x, my_y = my_q // NY, my_q % NY
    count = NZ * NQ
    right, left = lax.rem(me + 1, count), lax.rem(me + count - 1, count)
    in_plane = [
        lax.rem(my_x + dx, NX) * NY + lax.rem(my_y + dy, NY)
        for dx in range(NX) for dy in range(NY) if dx or dy
    ]
    in_line = [lax.rem(my_z + d, NZ) for d in range(1, NZ)]

    barrier = pltpu.get_barrier_semaphore()
    greet = [(left, core), (right, core), (me, 1 - core)]
    greet += [(my_z * NQ + q, core) for q in in_plane]
    greet += [(zz * NQ + my_q, core) for zz in in_line]
    for device in greet:
        pl.semaphore_signal(barrier, inc=1, device_id=device, device_id_type=MESH)
    load_x = pltpu.make_async_copy(x_ref, x, load.at[0])
    load_tiles = pltpu.make_async_copy(tiles_ref, tiles, load.at[1])
    load_x.start()
    load_tiles.start()
    load_x.wait()
    z[0, LOW : LOW + OWN, :] = x[...].astype(BF16)
    pl.semaphore_wait(barrier, len(greet))

    def remote(src, dst, send, recv, device):
        return pltpu.make_async_remote_copy(
            src_ref=src, dst_ref=dst, send_sem=send, recv_sem=recv,
            device_id=device, device_id_type=MESH,
        )

    def halo(s):
        down = remote(
            z.at[s, pl.ds(LOW, LOW)], z.at[s, pl.ds(LOW + OWN, LOW)],
            halo_s.at[s, 0], halo_r.at[s, 0], (left, core),
        )
        up = remote(
            z.at[s, pl.ds(OWN, LOW)], z.at[s, pl.ds(0, LOW)],
            halo_s.at[s, 1], halo_r.at[s, 1], (right, core),
        )
        return down, up

    def begin_halo(s):
        for copy in halo(s):
            copy.start()

    def band_dot(lanes, values):
        return dot(band[0, :, lanes], values, ((1,), (0,))) + dot(
            band[1, :, lanes], values, ((1,), (0,))
        )

    def apply(s):
        down, up = halo(s)
        product = band_dot(slice(LOW, LOW + OWN), z[s, LOW : LOW + OWN, :])
        up.wait_recv()
        product += band_dot(slice(0, LOW), z[s, 0:LOW, :])
        down.wait_recv()
        product += band_dot(slice(LOW + OWN, EXT), z[s, LOW + OWN : EXT, :])
        return product

    def send_on(s, value):
        z[s, LOW : LOW + OWN, :] = value.astype(BF16)
        begin_halo(s)

    begin_halo(0)
    load_tiles.wait()
    lowest = me * BR - CUT
    for r in range(BR):
        sums = [jnp.zeros((TILE, TILE), F32) for _ in range(SPAN)]
        for t in range(TPR):
            tile = tiles[r * TPR + t].astype(F32)
            place = cols_ref[r * TPR + t] - lowest
            for b in range(SPAN):
                sums[b] = sums[b] + jnp.where(place == b, tile, 0.0)
        for b in range(SPAN):
            high = sums[b].astype(BF16)
            rows = slice(r * TILE, (r + 1) * TILE)
            lanes = slice(b * TILE, (b + 1) * TILE)
            band[0, rows, lanes] = high
            band[1, rows, lanes] = (sums[b] - high.astype(F32)).astype(BF16)

    def sum_over_rows(it, part, plane, line, gram):
        for i, q in enumerate(in_plane):
            remote(
                part.at[it, q], plane.at[it, i + 1], plane_s.at[it], plane_r.at[it], (my_z * NQ + q, core)
            ).start()
        total = part[it, my_q]
        rest = pl.ds(1, NQ - 1)
        all_of_plane = remote(plane.at[it, rest], plane.at[it, rest], plane_s.at[it], plane_r.at[it], (me, 1 - core))
        all_of_plane.wait_recv()
        for i in range(1, NQ):
            total += plane[it, i]
        line[it, my_z] = total
        mine = line.at[it, my_z]
        for zz in in_line:
            remote(mine, mine, line_s.at[it], line_r.at[it], (zz * NQ + my_q, core)).start()
        rest = pl.ds(0, NZ - 1)
        all_of_line = remote(line.at[it, rest], line.at[it, rest], line_s.at[it], line_r.at[it], (me, 1 - core))
        all_of_line.wait_recv()
        total = line[it, 0]
        for i in range(1, NZ):
            total += line[it, i]
        gram[it, my_q] = total / (count * OWN)
        mine = gram.at[it, my_q]
        for q in in_plane:
            remote(mine, mine, gram_s.at[it], gram_r.at[it], (my_z * NQ + q, core)).start()
        rest = pl.ds(0, NQ - 1)
        all_of_gram = remote(gram.at[it, rest], gram.at[it, rest], gram_s.at[it], gram_r.at[it], (me, 1 - core))
        all_of_gram.wait_recv()
        for copy in (all_of_plane, all_of_line, all_of_gram):
            copy.wait_send()

    def iteration(it, carry):
        first = it * DEGREE

        @pl.when(it > 0)
        def _():
            send_on(first, x[...])

        y1[...] = ((1.0 - 1.25) * x[...] - apply(first)) / 0.75
        send_on(first + 1, y1[...])
        y2[...] = 2.0 * ((1.0 - 1.25) * y1[...] - apply(first + 1)) / 0.75 - x[...]
        send_on(first + 2, y2[...])
        y3[it] = 2.0 * ((1.0 - 1.25) * y2[...] - apply(first + 2)) / 0.75 - y1[...]
        give_y = remote(y3.at[it], other.at[it], pair_s.at[it, 0], pair_r.at[it, 0], (me, 1))
        give_w = remote(w.at[it], waa.at[it], pair_s.at[it, 1], pair_r.at[it, 1], (me, 1))
        take_y = remote(y3.at[it], other.at[it], pair_s.at[it, 0], pair_r.at[it, 0], (me, 0))
        take_w = remote(w.at[it], waa.at[it], pair_s.at[it, 1], pair_r.at[it, 1], (me, 0))
        rows_a, rows_b = TILE // NQ, 2 * TILE // NQ

        @pl.when(core == 0)
        def _():
            give_y.start()
            y = y3[it]
            block = dot(y, y, ((0,), (0,)), HIGHEST)
            for q in range(NQ):
                part_a[it, q] = block[rows_a * q : rows_a * (q + 1), :]
            sum_over_rows(it, part_a, plane_a, line_a, gram_a)
            for q in range(NQ):
                m[rows_a * q : rows_a * (q + 1), :] = gram_a[it, q]

        @pl.when(core == 1)
        def _():
            y = y3[it]
            block = dot(y, y, ((0,), (0,)), HIGHEST)
            for q in range(NQ // 2):
                part_b[it, NQ // 2 + q] = block[rows_b * q : rows_b * (q + 1), :]
            take_y.wait_recv()
            block = dot(other[it], y, ((0,), (0,)), HIGHEST)
            for q in range(NQ // 2):
                part_b[it, q] = block[rows_b * q : rows_b * (q + 1), :]
            sum_over_rows(it, part_b, plane_b, line_b, gram_b)
            take_w.wait_recv()
            gab = gram_b[it, 0 : NQ // 2].reshape(TILE, TILE)
            gbb = gram_b[it, NQ // 2 :].reshape(TILE, TILE)
            cab = dot(waa[it], gab, ((1,), (0,)), HIGHEST)
            m[...] = gbb - dot(cab, cab, ((0,), (0,)), HIGHEST)
            shift = dot(waa[it], cab, ((0,), (0,)), HIGHEST)
            y3[it] = y - dot(other[it], shift, ((1,), (0,)), HIGHEST)

        for g, group in enumerate(inverse_factor([m[8 * i : 8 * i + 8, :] for i in range(16)])):
            w[it, 8 * g : 8 * g + 8, :] = group

        @pl.when(core == 0)
        def _():
            give_w.start()

        x[...] = dot(y3[it], w[it], ((1,), (1,)), HIGHEST)

        @pl.when(core == 0)
        def _():
            give_y.wait_send()
            give_w.wait_send()

        for step in range(DEGREE):
            for copy in halo(first + step):
                copy.wait_send()
        return carry

    lax.fori_loop(0, ITERS, iteration, 0)
    out_ref[...] = x[...]


def per_device(axes, start, tiles, tile_cols):
    NZ, NX, NY = axes
    NQ = NX * NY
    rows_a, rows_b = TILE // NQ, 2 * TILE // NQ
    dma = pltpu.SemaphoreType.DMA
    steps = ITERS * DEGREE

    def vmem(*shape, dtype=F32):
        return pltpu.VMEM(shape, dtype)

    return pl.pallas_call(
        functools.partial(kernel, axes),
        out_shape=jax.ShapeDtypeStruct((OWN, TILE), F32),
        in_specs=[pl.BlockSpec(memory_space=pltpu.SMEM), ANY, ANY],
        out_specs=pl.BlockSpec(memory_space=pltpu.VMEM),
        scratch_shapes=[
            vmem(BR * TPR, TILE, TILE, dtype=BF16),
            vmem(2, OWN, EXT, dtype=BF16),
            vmem(OWN, TILE),
            vmem(steps, EXT, TILE, dtype=BF16),
            vmem(OWN, TILE), vmem(OWN, TILE), vmem(ITERS, OWN, TILE), vmem(ITERS, OWN, TILE),
            vmem(TILE, TILE), vmem(ITERS, TILE, TILE), vmem(ITERS, TILE, TILE),
            vmem(ITERS, NQ, rows_a, TILE), vmem(ITERS, NQ, rows_b, TILE),
            vmem(ITERS, NQ, rows_a, TILE), vmem(ITERS, NQ, rows_b, TILE),
            vmem(ITERS, NZ, rows_a, TILE), vmem(ITERS, NZ, rows_b, TILE),
            vmem(ITERS, NQ, rows_a, TILE), vmem(ITERS, NQ, rows_b, TILE),
            dma((2,)), dma((steps, 2)), dma((steps, 2)), dma((ITERS, 2)), dma((ITERS, 2)),
        ] + [dma((ITERS,))] * 6,
        compiler_params=pltpu.CompilerParams(collective_id=0, has_side_effects=True),
        name="embed",
    )(tile_cols, start, tiles)


def solution(mesh, axes=AXES):
    placed = (P("rows", "cols"), P("rows", None, None), P("rows"))
    return jax.shard_map(
        functools.partial(per_device, axes),
        mesh=mesh, in_specs=placed, out_specs=P("rows", "cols"), check_vma=False,
    )
```

time: 999 us -> 114 us (0.11)
  waiting for transfers between devices: 783 us -> 0 us
  other arithmetic: 113 us -> 0 us
  Pallas kernels: 0 us -> 112 us
  starting transfers between devices: 30.3 us -> 0 us
  blocking collectives: 21.5 us -> 0 us
  between operations: 16.8 us -> 0.01 us
  local copies, waits for them, and re-layouts: 13.6 us -> 1.62 us
  matrix products: 10.3 us -> 0 us
    psum x2 -> x0, waiting for transfers between devices: 760 us -> none  [per_device(): gram = lax.psum(partial_gram, 'rows') / node_count]
    pallas_call x0 -> x1, Pallas kernels: none -> 112 us  [per_device(): pl.pallas_call(functools.partial(kernel, axes), out_shape=jax.ShapeDtypeS...]
    another operation x18 -> x0, other arithmetic: 108 us -> none  [the longest x13 68.7 us: per_device(): factor = jnp.linalg.cholesky(gram)]
    ppermute x12 -> x0, starting transfers between devices: 30 us -> none  [the longest x6 22.3 us: extended_2(): lax.ppermute(lax.slice_in_dim(block, block.shape[dim] - width, None, axis...]
    ppermute x12 -> x0, waiting for transfers between devices: 23 us -> none  [the longest x6 23 us: extended_2(): lax.ppermute(lax.slice_in_dim(block, 0, width, axis=dim), axis, backward)]
    all_gather x2 -> x0, blocking collectives: 21.5 us -> none  [per_device(): full_panel = lax.all_gather(y_curr, 'cols', axis=1, tiled=True)]
  transfers between devices with their start and end apart: 14 -> 0, of which waited for: 8 -> 0; matrix products, arithmetic and copies ran while one was open for 0% -> 0% of each run, Pallas kernels for 0% -> 0%
where the time goes in v2:
time: 114 us
  Pallas kernels  112 us (98%)
  local copies, waits for them, and re-layouts  1.62 us (1%)
    pallas_call x1, Pallas kernels, per_device(): pl.pallas_call(functools.partial(kernel, axes), out_shape=jax.ShapeDtypeS...  112 us

profile of v2, /device:TPU:1, one launch (start us, length us, event | category | flops | bytes accessed | tf_op | source)
XLA Modules:
  0.0 113.6 jit_solution(17861193869964697735)
XLA Ops:
  0.0 111.9 %embed.1 = f32[384,128]{1,0:T(8,128)} custom-call(s32[36]{0:T(128)} %cols_ref.1, f32[384,128]{1,0:T(8,128)} %x_ref.1, bf16[36,128,128]{2,1,0:T(8,128)(2,1)} %tiles_ref.1), custom_call_target="tpu_custom_call" | custom-call | tf_op jit(solution)/shard_map/embed/pallas_call | solution.py:285
  111.9 1.6 %copy.5 = f32[384,128]{1,0:T(8,128)} copy(f32[384,128]{1,0:T(8,128)} %embed.1) | data formatting | bytes 393216

commit v3 on v2

--- a/solution.py
+++ b/solution.py
@@ -82,9 +82,9 @@
 
 def kernel(
     axes, cols_ref, x_ref, tiles_ref, out_ref,
-    tiles, band, x, z, y1, y2, y3, other, m, w, waa,
+    tiles, band, x, z, y1, y2, y3, other, m, w, waa, shift, wba,
     part_a, part_b, plane_a, plane_b, line_a, line_b, gram_a, gram_b,
-    load, halo_s, halo_r, pair_s, pair_r, plane_s, plane_r, line_s, line_r, gram_s, gram_r,
+    load, halo_s, halo_r, pair_s, pair_r, edge_s, edge_r, pass_s, pass_r, plane_s, plane_r, line_s, line_r, gram_s, gram_r,
 ):
     NZ, NX, NY = axes
     NQ = NX * NY
@@ -94,11 +94,14 @@
     my_x, my_y = my_q // NY, my_q % NY
     count = NZ * NQ
     right, left = lax.rem(me + 1, count), lax.rem(me + count - 1, count)
-    in_plane = [
-        lax.rem(my_x + dx, NX) * NY + lax.rem(my_y + dy, NY)
-        for dx in range(NX) for dy in range(NY) if dx or dy
-    ]
-    in_line = [lax.rem(my_z + d, NZ) for d in range(1, NZ)]
+    steps = [(dx, dy) for dx in range(NX) for dy in range(NY) if dx or dy]
+    steps.sort(key=lambda s: -min(s[0], NX - s[0]) - min(s[1], NY - s[1]))
+    in_plane = [lax.rem(my_x + dx, NX) * NY + lax.rem(my_y + dy, NY) for dx, dy in steps]
+    in_line = [lax.rem(my_z + d, NZ) for d in sorted(range(1, NZ), key=lambda d: -min(d, NZ - d))]
+    load_x = pltpu.make_async_copy(x_ref, x, load.at[0])
+    load_tiles = pltpu.make_async_copy(tiles_ref, tiles, load.at[1])
+    load_x.start()
+    load_tiles.start()
 
     barrier = pltpu.get_barrier_semaphore()
     greet = [(left, core), (right, core), (me, 1 - core)]
@@ -106,10 +109,6 @@
     greet += [(zz * NQ + my_q, core) for zz in in_line]
     for device in greet:
         pl.semaphore_signal(barrier, inc=1, device_id=device, device_id_type=MESH)
-    load_x = pltpu.make_async_copy(x_ref, x, load.at[0])
-    load_tiles = pltpu.make_async_copy(tiles_ref, tiles, load.at[1])
-    load_x.start()
-    load_tiles.start()
     load_x.wait()
     z[0, LOW : LOW + OWN, :] = x[...].astype(BF16)
     pl.semaphore_wait(barrier, len(greet))
@@ -120,6 +119,19 @@
             device_id=device, device_id_type=MESH,
         )
 
+    def edges():
+        down = remote(
+            y3.at[0, pl.ds(LOW, LOW)], y3.at[0, pl.ds(LOW + OWN, LOW)], edge_s.at[0], edge_r.at[0], (left, core)
+        )
+        up = remote(y3.at[0, pl.ds(OWN, LOW)], y3.at[0, pl.ds(0, LOW)], edge_s.at[1], edge_r.at[1], (right, core))
+        return down, up
+
+    def passes(device):
+        return [
+            remote(y3.at[0, rows], other.at[0, rows], pass_s.at[i], pass_r.at[i], device)
+            for i, rows in enumerate((pl.ds(0, LOW), pl.ds(LOW + OWN, LOW)))
+        ]
+
     def halo(s):
         down = remote(
             z.at[s, pl.ds(LOW, LOW)], z.at[s, pl.ds(LOW + OWN, LOW)],
@@ -140,12 +152,12 @@
             band[1, :, lanes], values, ((1,), (0,))
         )
 
-    def apply(s):
+    def apply(s, travelled=True):
         down, up = halo(s)
         product = band_dot(slice(LOW, LOW + OWN), z[s, LOW : LOW + OWN, :])
-        up.wait_recv()
+        pl.when(travelled)(up.wait_recv)
         product += band_dot(slice(0, LOW), z[s, 0:LOW, :])
-        down.wait_recv()
+        pl.when(travelled)(down.wait_recv)
         product += band_dot(slice(LOW + OWN, EXT), z[s, LOW + OWN : EXT, :])
         return product
 
@@ -185,6 +197,12 @@
         mine = line.at[it, my_z]
         for zz in in_line:
             remote(mine, mine, line_s.at[it], line_r.at[it], (zz * NQ + my_q, core)).start()
+
+        @pl.when(it == 0)
+        def _():
+            for copy in edges():
+                copy.start()
+
         rest = pl.ds(0, NZ - 1)
         all_of_line = remote(line.at[it, rest], line.at[it, rest], line_s.at[it], line_r.at[it], (me, 1 - core))
         all_of_line.wait_recv()
@@ -204,25 +222,22 @@
     def iteration(it, carry):
         first = it * DEGREE
 
-        @pl.when(it > 0)
-        def _():
-            send_on(first, x[...])
-
-        y1[...] = ((1.0 - 1.25) * x[...] - apply(first)) / 0.75
+        own = slice(LOW, LOW + OWN)
+        y1[...] = ((1.0 - 1.25) * x[...] - apply(first, it == 0)) / 0.75
         send_on(first + 1, y1[...])
         y2[...] = 2.0 * ((1.0 - 1.25) * y1[...] - apply(first + 1)) / 0.75 - x[...]
         send_on(first + 2, y2[...])
-        y3[it] = 2.0 * ((1.0 - 1.25) * y2[...] - apply(first + 2)) / 0.75 - y1[...]
-        give_y = remote(y3.at[it], other.at[it], pair_s.at[it, 0], pair_r.at[it, 0], (me, 1))
+        y3[it, own, :] = 2.0 * ((1.0 - 1.25) * y2[...] - apply(first + 2)) / 0.75 - y1[...]
+        give_y = remote(y3.at[it, pl.ds(LOW, OWN)], other.at[it, pl.ds(LOW, OWN)], pair_s.at[it, 0], pair_r.at[it, 0], (me, 1))
         give_w = remote(w.at[it], waa.at[it], pair_s.at[it, 1], pair_r.at[it, 1], (me, 1))
-        take_y = remote(y3.at[it], other.at[it], pair_s.at[it, 0], pair_r.at[it, 0], (me, 0))
+        take_y = remote(y3.at[it, pl.ds(LOW, OWN)], other.at[it, pl.ds(LOW, OWN)], pair_s.at[it, 0], pair_r.at[it, 0], (me, 0))
         take_w = remote(w.at[it], waa.at[it], pair_s.at[it, 1], pair_r.at[it, 1], (me, 0))
         rows_a, rows_b = TILE // NQ, 2 * TILE // NQ
 
         @pl.when(core == 0)
         def _():
             give_y.start()
-            y = y3[it]
+            y = y3[it, own, :]
             block = dot(y, y, ((0,), (0,)), HIGHEST)
             for q in range(NQ):
                 part_a[it, q] = block[rows_a * q : rows_a * (q + 1), :]
@@ -230,14 +245,21 @@
             for q in range(NQ):
                 m[rows_a * q : rows_a * (q + 1), :] = gram_a[it, q]
 
+            @pl.when(it == 0)
+            def _():
+                for copy in edges():
+                    copy.wait_recv()
+                for copy in passes((me, 1)):
+                    copy.start()
+
         @pl.when(core == 1)
         def _():
-            y = y3[it]
+            y = y3[it, own, :]
             block = dot(y, y, ((0,), (0,)), HIGHEST)
             for q in range(NQ // 2):
                 part_b[it, NQ // 2 + q] = block[rows_b * q : rows_b * (q + 1), :]
             take_y.wait_recv()
-            block = dot(other[it], y, ((0,), (0,)), HIGHEST)
+            block = dot(other[it, own, :], y, ((0,), (0,)), HIGHEST)
             for q in range(NQ // 2):
                 part_b[it, q] = block[rows_b * q : rows_b * (q + 1), :]
             sum_over_rows(it, part_b, plane_b, line_b, gram_b)
@@ -246,24 +268,53 @@
             gbb = gram_b[it, NQ // 2 :].reshape(TILE, TILE)
             cab = dot(waa[it], gab, ((1,), (0,)), HIGHEST)
             m[...] = gbb - dot(cab, cab, ((0,), (0,)), HIGHEST)
-            shift = dot(waa[it], cab, ((0,), (0,)), HIGHEST)
-            y3[it] = y - dot(other[it], shift, ((1,), (0,)), HIGHEST)
+            shift[...] = dot(waa[it], cab, ((0,), (0,)), HIGHEST)
 
         for g, group in enumerate(inverse_factor([m[8 * i : 8 * i + 8, :] for i in range(16)])):
             w[it, 8 * g : 8 * g + 8, :] = group
 
+        def update(new_rows, arrive):
+            x[...] = new_rows(own)
+
+            @pl.when(it == 0)
+            def _():
+                z[DEGREE, own, :] = x[...].astype(BF16)
+                arrive()
+                for rows in (slice(0, LOW), slice(LOW + OWN, EXT)):
+                    z[DEGREE, rows, :] = new_rows(rows).astype(BF16)
+
         @pl.when(core == 0)
         def _():
             give_w.start()
-
-        x[...] = dot(y3[it], w[it], ((1,), (1,)), HIGHEST)
-
-        @pl.when(core == 0)
-        def _():
+            update(lambda rows: dot(y3[it, rows, :], w[it], ((1,), (1,)), HIGHEST), lambda: None)
             give_y.wait_send()
             give_w.wait_send()
 
-        for step in range(DEGREE):
+            @pl.when(it == 0)
+            def _():
+                for copy in passes((me, 1)):
+                    copy.wait_send()
+
+        @pl.when(core == 1)
+        def _():
+            wba[...] = -dot(w[it], shift[...], ((1,), (1,)), HIGHEST)
+
+            def new_rows(rows):
+                both = jnp.concatenate([y3[it, rows, :], other[it, rows, :]], axis=1)
+                return dot(both, jnp.concatenate([w[it], wba[...]], axis=1), ((1,), (1,)), HIGHEST)
+
+            def arrive():
+                for copy in [*edges(), *passes((me, 0))]:
+                    copy.wait_recv()
+
+            update(new_rows, arrive)
+
+        @pl.when(it == 0)
+        def _():
+            for copy in [*halo(0), *edges()]:
+                copy.wait_send()
+
+        for step in range(1, DEGREE):
             for copy in halo(first + step):
                 copy.wait_send()
         return carry
@@ -292,13 +343,14 @@
             vmem(2, OWN, EXT, dtype=BF16),
             vmem(OWN, TILE),
             vmem(steps, EXT, TILE, dtype=BF16),
-            vmem(OWN, TILE), vmem(OWN, TILE), vmem(ITERS, OWN, TILE), vmem(ITERS, OWN, TILE),
-            vmem(TILE, TILE), vmem(ITERS, TILE, TILE), vmem(ITERS, TILE, TILE),
+            vmem(OWN, TILE), vmem(OWN, TILE), vmem(ITERS, EXT, TILE), vmem(ITERS, EXT, TILE),
+            vmem(TILE, TILE), vmem(ITERS, TILE, TILE), vmem(ITERS, TILE, TILE), vmem(TILE, TILE), vmem(TILE, TILE),
             vmem(ITERS, NQ, rows_a, TILE), vmem(ITERS, NQ, rows_b, TILE),
             vmem(ITERS, NQ, rows_a, TILE), vmem(ITERS, NQ, rows_b, TILE),
             vmem(ITERS, NZ, rows_a, TILE), vmem(ITERS, NZ, rows_b, TILE),
             vmem(ITERS, NQ, rows_a, TILE), vmem(ITERS, NQ, rows_b, TILE),
             dma((2,)), dma((steps, 2)), dma((steps, 2)), dma((ITERS, 2)), dma((ITERS, 2)),
+            dma((2,)), dma((2,)), dma((2,)), dma((2,)),
         ] + [dma((ITERS,))] * 6,
         compiler_params=pltpu.CompilerParams(collective_id=0, has_side_effects=True),
         name="embed",

time: 114 us -> 107 us (0.939)
  Pallas kernels: 112 us -> 105 us
    pallas_call x1, Pallas kernels: 112 us -> 105 us  [per_device(): pl.pallas_call(functools.partial(kernel, axes), out_shape=jax.ShapeDtypeS...]
where the time goes in v3:
time: 107 us; the launch traced here: 106 us
  Pallas kernels  105 us (98%)
  local copies, waits for them, and re-layouts  1.62 us (2%)
    pallas_call x1, Pallas kernels, per_device(): pl.pallas_call(functools.partial(kernel, axes), out_shape=jax.ShapeDtypeS...  105 us

profile of v3, /device:TPU:1, one launch (start us, length us, event | category | flops | bytes accessed | tf_op | source)
XLA Modules:
  0.0 106.4 jit_solution(10372588917303478409)
XLA Ops:
  0.0 104.8 %embed.1 = f32[384,128]{1,0:T(8,128)} custom-call(s32[36]{0:T(128)} %cols_ref.1, f32[384,128]{1,0:T(8,128)} %x_ref.1, bf16[36,128,128]{2,1,0:T(8,128)(2,1)} %tiles_ref.1), custom_call_target="tpu_custom_call" | custom-call | tf_op jit(solution)/shard_map/embed/pallas_call | solution.py:336
  104.8 1.6 %copy.5 = f32[384,128]{1,0:T(8,128)} copy(f32[384,128]{1,0:T(8,128)} %embed.1) | data formatting | bytes 393216

commit v4 on v3

--- a/solution.py
+++ b/solution.py
@@ -81,10 +81,10 @@
 
 
 def kernel(
-    axes, cols_ref, x_ref, tiles_ref, out_ref,
+    axes, cols_ref, x_ref, tiles_ref, last_y, last_w,
     tiles, band, x, z, y1, y2, y3, other, m, w, waa, shift, wba,
     part_a, part_b, plane_a, plane_b, line_a, line_b, gram_a, gram_b,
-    load, halo_s, halo_r, pair_s, pair_r, edge_s, edge_r, pass_s, pass_r, plane_s, plane_r, line_s, line_r, gram_s, gram_r,
+    load, store, halo_s, halo_r, pair_s, pair_r, edge_s, edge_r, pass_s, pass_r, plane_s, plane_r, line_s, line_r, gram_s, gram_r,
 ):
     NZ, NX, NY = axes
     NQ = NX * NY
@@ -94,6 +94,7 @@
     my_x, my_y = my_q // NY, my_q % NY
     count = NZ * NQ
     right, left = lax.rem(me + 1, count), lax.rem(me + count - 1, count)
+    has_left, has_right = me > 0, me < count - 1
     steps = [(dx, dy) for dx in range(NX) for dy in range(NY) if dx or dy]
     steps.sort(key=lambda s: -min(s[0], NX - s[0]) - min(s[1], NY - s[1]))
     in_plane = [lax.rem(my_x + dx, NX) * NY + lax.rem(my_y + dy, NY) for dx, dy in steps]
@@ -104,11 +105,27 @@
     load_tiles.start()
 
     barrier = pltpu.get_barrier_semaphore()
-    greet = [(left, core), (right, core), (me, 1 - core)]
+    greet = [(zz * NQ + my_q, core) for zz in in_line]
     greet += [(my_z * NQ + q, core) for q in in_plane]
-    greet += [(zz * NQ + my_q, core) for zz in in_line]
+    greet += [(left, core), (right, core), (me, 1 - core)]
     for device in greet:
         pl.semaphore_signal(barrier, inc=1, device_id=device, device_id_type=MESH)
+
+    @pl.when(me == 0)
+    def _():
+        z[:, 0:LOW, :] = jnp.zeros((ITERS * DEGREE, LOW, TILE), BF16)
+        y3[0, 0:LOW, :] = jnp.zeros((LOW, TILE), F32)
+
+    @pl.when(me == count - 1)
+    def _():
+        z[:, LOW + OWN : EXT, :] = jnp.zeros((ITERS * DEGREE, LOW, TILE), BF16)
+        y3[0, LOW + OWN : EXT, :] = jnp.zeros((LOW, TILE), F32)
+
+    @pl.when(core == 0)
+    def _():
+        other[ITERS - 1, LOW : LOW + OWN, :] = jnp.zeros((OWN, TILE), F32)
+        wba[...] = jnp.zeros((TILE, TILE), F32)
+
     load_x.wait()
     z[0, LOW : LOW + OWN, :] = x[...].astype(BF16)
     pl.semaphore_wait(barrier, len(greet))
@@ -143,9 +160,17 @@
         )
         return down, up
 
-    def begin_halo(s):
-        for copy in halo(s):
-            copy.start()
+    def begin(pair):
+        pl.when(has_left)(pair[0].start)
+        pl.when(has_right)(pair[1].start)
+
+    def sent(pair):
+        pl.when(has_left)(pair[0].wait_send)
+        pl.when(has_right)(pair[1].wait_send)
+
+    def arrived(pair):
+        pl.when(has_right)(pair[0].wait_recv)
+        pl.when(has_left)(pair[1].wait_recv)
 
     def band_dot(lanes, values):
         return dot(band[0, :, lanes], values, ((1,), (0,))) + dot(
@@ -155,17 +180,17 @@
     def apply(s, travelled=True):
         down, up = halo(s)
         product = band_dot(slice(LOW, LOW + OWN), z[s, LOW : LOW + OWN, :])
-        pl.when(travelled)(up.wait_recv)
+        pl.when(jnp.logical_and(travelled, has_left))(up.wait_recv)
         product += band_dot(slice(0, LOW), z[s, 0:LOW, :])
-        pl.when(travelled)(down.wait_recv)
+        pl.when(jnp.logical_and(travelled, has_right))(down.wait_recv)
         product += band_dot(slice(LOW + OWN, EXT), z[s, LOW + OWN : EXT, :])
         return product
 
     def send_on(s, value):
         z[s, LOW : LOW + OWN, :] = value.astype(BF16)
-        begin_halo(s)
-
-    begin_halo(0)
+        begin(halo(s))
+
+    begin(halo(0))
     load_tiles.wait()
     lowest = me * BR - CUT
     for r in range(BR):
@@ -200,8 +225,7 @@
 
         @pl.when(it == 0)
         def _():
-            for copy in edges():
-                copy.start()
+            begin(edges())
 
         rest = pl.ds(0, NZ - 1)
         all_of_line = remote(line.at[it, rest], line.at[it, rest], line_s.at[it], line_r.at[it], (me, 1 - core))
@@ -247,8 +271,7 @@
 
             @pl.when(it == 0)
             def _():
-                for copy in edges():
-                    copy.wait_recv()
+                arrived(edges())
                 for copy in passes((me, 1)):
                     copy.start()
 
@@ -270,14 +293,29 @@
             m[...] = gbb - dot(cab, cab, ((0,), (0,)), HIGHEST)
             shift[...] = dot(waa[it], cab, ((0,), (0,)), HIGHEST)
 
+        own_rows = pl.ds(LOW, OWN)
+        first_half, second_half = pl.ds(0, TILE), pl.ds(TILE, TILE)
+        stores = [
+            pltpu.make_async_copy(y3.at[ITERS - 1, own_rows], last_y.at[:, first_half], store.at[0]),
+            pltpu.make_async_copy(other.at[ITERS - 1, own_rows], last_y.at[:, second_half], store.at[1]),
+            pltpu.make_async_copy(w.at[ITERS - 1], last_w.at[:, first_half], store.at[2]),
+            pltpu.make_async_copy(wba, last_w.at[:, second_half], store.at[3]),
+        ]
+
+        @pl.when(it == ITERS - 1)
+        def _():
+            stores[0].start()
+            stores[1].start()
+
         for g, group in enumerate(inverse_factor([m[8 * i : 8 * i + 8, :] for i in range(16)])):
             w[it, 8 * g : 8 * g + 8, :] = group
 
+        pl.when(it == ITERS - 1)(stores[2].start)
+
         def update(new_rows, arrive):
-            x[...] = new_rows(own)
-
             @pl.when(it == 0)
             def _():
+                x[...] = new_rows(own)
                 z[DEGREE, own, :] = x[...].astype(BF16)
                 arrive()
                 for rows in (slice(0, LOW), slice(LOW + OWN, EXT)):
@@ -304,23 +342,28 @@
                 return dot(both, jnp.concatenate([w[it], wba[...]], axis=1), ((1,), (1,)), HIGHEST)
 
             def arrive():
-                for copy in [*edges(), *passes((me, 0))]:
+                arrived(edges())
+                for copy in passes((me, 0)):
                     copy.wait_recv()
 
             update(new_rows, arrive)
 
+        @pl.when(it == ITERS - 1)
+        def _():
+            stores[3].start()
+            for copy in stores:
+                copy.wait()
+
         @pl.when(it == 0)
         def _():
-            for copy in [*halo(0), *edges()]:
-                copy.wait_send()
+            sent(halo(0))
+            sent(edges())
 
         for step in range(1, DEGREE):
-            for copy in halo(first + step):
-                copy.wait_send()
+            sent(halo(first + step))
         return carry
 
     lax.fori_loop(0, ITERS, iteration, 0)
-    out_ref[...] = x[...]
 
 
 def per_device(axes, start, tiles, tile_cols):
@@ -333,11 +376,11 @@
     def vmem(*shape, dtype=F32):
         return pltpu.VMEM(shape, dtype)
 
-    return pl.pallas_call(
+    last_y, last_w = pl.pallas_call(
         functools.partial(kernel, axes),
-        out_shape=jax.ShapeDtypeStruct((OWN, TILE), F32),
+        out_shape=(jax.ShapeDtypeStruct((OWN, 2 * TILE), F32), jax.ShapeDtypeStruct((TILE, 2 * TILE), F32)),
         in_specs=[pl.BlockSpec(memory_space=pltpu.SMEM), ANY, ANY],
-        out_specs=pl.BlockSpec(memory_space=pltpu.VMEM),
+        out_specs=(ANY, ANY),
         scratch_shapes=[
             vmem(BR * TPR, TILE, TILE, dtype=BF16),
             vmem(2, OWN, EXT, dtype=BF16),
@@ -349,12 +392,13 @@
             vmem(ITERS, NQ, rows_a, TILE), vmem(ITERS, NQ, rows_b, TILE),
             vmem(ITERS, NZ, rows_a, TILE), vmem(ITERS, NZ, rows_b, TILE),
             vmem(ITERS, NQ, rows_a, TILE), vmem(ITERS, NQ, rows_b, TILE),
-            dma((2,)), dma((steps, 2)), dma((steps, 2)), dma((ITERS, 2)), dma((ITERS, 2)),
+            dma((2,)), dma((4,)), dma((steps, 2)), dma((steps, 2)), dma((ITERS, 2)), dma((ITERS, 2)),
             dma((2,)), dma((2,)), dma((2,)), dma((2,)),
         ] + [dma((ITERS,))] * 6,
         compiler_params=pltpu.CompilerParams(collective_id=0, has_side_effects=True),
         name="embed",
     )(tile_cols, start, tiles)
+    return dot(last_y, last_w, ((1,), (1,)), HIGHEST)
 
 
 def solution(mesh, axes=AXES):

time: 107 us -> 105 us (0.981)
  matrix products: 0 us -> 2.18 us
  Pallas kernels: 105 us -> 103 us
  local copies, waits for them, and re-layouts: 1.62 us -> 0 us
    dot_general x0 -> x1, matrix products: none -> 2.18 us  [dot(): lax.dot_general(a, b, (contract, ((), ())), precision=precision, preferre...]
    pallas_call x1, Pallas kernels: 105 us -> 103 us  [per_device(): pl.pallas_call(functools.partial(kernel, axes), out_shape=(jax.ShapeDtype...]
    unnamed x1 -> x0, local copies, waits for them, and re-layouts: 1.62 us -> none
where the time goes in v4:
time: 105 us
  Pallas kernels  103 us (98%)
  matrix products  2.18 us (2%)
    pallas_call x1, Pallas kernels, per_device(): pl.pallas_call(functools.partial(kernel, axes), out_shape=(jax.ShapeDtype...  103 us
    dot_general x1, matrix products, dot(): lax.dot_general(a, b, (contract, ((), ())), precision=precision, preferre...  2.18 us

profile of v4, /device:TPU:1, one launch (start us, length us, event | category | flops | bytes accessed | tf_op | source)
XLA Modules:
  0.0 105.1 jit_solution(6469783372437114932)
XLA Ops:
  0.0 102.9 %embed.1 = (f32[384,256]{1,0:T(8,128)}, f32[128,256]{1,0:T(8,128)}) custom-call(s32[36]{0:T(128)} %cols_ref.1, f32[384,128]{1,0:T(8,128)} %x_ref.1, bf16[36,128,128]{2,1,0:T(8,128)(2,1)} %tiles_ref.1), custom_call_target="tpu_custom_call" | custom-call | tf_op jit(solution)/shard_map/embed/pallas_call | solution.py:379
  102.9 2.2 %fusion = f32[384,128]{1,0:T(8,128)} fusion(f32[384,256]{1,0:T(8,128)} %get-tuple-element.7, f32[128,256]{1,0:T(8,128)} %get-tuple-element.8), kind=kOutput, calls=%fused_computation | convolution fusion | flops 150994944 | bytes 720896 | tf_op jit(solution)/shard_map/dot_general | solution.py:29

commit v5 on v4

--- a/solution.py
+++ b/solution.py
@@ -80,9 +80,13 @@
     return w
 
 
+def clear(ref, rows):
+    ref[ITERS - 1, rows, :] = jnp.zeros((LOW, TILE), F32)
+
+
 def kernel(
-    axes, cols_ref, x_ref, tiles_ref, last_y, last_w,
-    tiles, band, x, z, y1, y2, y3, other, m, w, waa, shift, wba,
+    axes, cols_hbm, x_ref, tiles_ref, last_y, last_w,
+    cols_ref, tiles, band, x, z, y1, y2, y3, other, m, w, waa, cab, rest,
     part_a, part_b, plane_a, plane_b, line_a, line_b, gram_a, gram_b,
     load, store, halo_s, halo_r, pair_s, pair_r, edge_s, edge_r, pass_s, pass_r, plane_s, plane_r, line_s, line_r, gram_s, gram_r,
 ):
@@ -101,7 +105,9 @@
     in_line = [lax.rem(my_z + d, NZ) for d in sorted(range(1, NZ), key=lambda d: -min(d, NZ - d))]
     load_x = pltpu.make_async_copy(x_ref, x, load.at[0])
     load_tiles = pltpu.make_async_copy(tiles_ref, tiles, load.at[1])
+    load_cols = pltpu.make_async_copy(cols_hbm, cols_ref, load.at[2])
     load_x.start()
+    load_cols.start()
     load_tiles.start()
 
     barrier = pltpu.get_barrier_semaphore()
@@ -120,11 +126,6 @@
     def _():
         z[:, LOW + OWN : EXT, :] = jnp.zeros((ITERS * DEGREE, LOW, TILE), BF16)
         y3[0, LOW + OWN : EXT, :] = jnp.zeros((LOW, TILE), F32)
-
-    @pl.when(core == 0)
-    def _():
-        other[ITERS - 1, LOW : LOW + OWN, :] = jnp.zeros((OWN, TILE), F32)
-        wba[...] = jnp.zeros((TILE, TILE), F32)
 
     load_x.wait()
     z[0, LOW : LOW + OWN, :] = x[...].astype(BF16)
@@ -191,6 +192,17 @@
         begin(halo(s))
 
     begin(halo(0))
+
+    @pl.when(core == 0)
+    def _():
+        other[...] = jnp.zeros((ITERS, EXT, TILE), F32)
+        waa[...] = jnp.zeros((ITERS, TILE, TILE), F32)
+        cab[...] = jnp.zeros((TILE, TILE), F32)
+
+    for rows in (slice(0, LOW), slice(LOW + OWN, EXT)):
+        y3[ITERS - 1, rows, :] = jnp.zeros((LOW, TILE), F32)
+        pl.when(core == 1)(functools.partial(clear, other, rows))
+    load_cols.wait()
     load_tiles.wait()
     lowest = me * BR - CUT
     for r in range(BR):
@@ -289,42 +301,41 @@
             take_w.wait_recv()
             gab = gram_b[it, 0 : NQ // 2].reshape(TILE, TILE)
             gbb = gram_b[it, NQ // 2 :].reshape(TILE, TILE)
-            cab = dot(waa[it], gab, ((1,), (0,)), HIGHEST)
-            m[...] = gbb - dot(cab, cab, ((0,), (0,)), HIGHEST)
-            shift[...] = dot(waa[it], cab, ((0,), (0,)), HIGHEST)
-
-        own_rows = pl.ds(LOW, OWN)
-        first_half, second_half = pl.ds(0, TILE), pl.ds(TILE, TILE)
-        stores = [
-            pltpu.make_async_copy(y3.at[ITERS - 1, own_rows], last_y.at[:, first_half], store.at[0]),
-            pltpu.make_async_copy(other.at[ITERS - 1, own_rows], last_y.at[:, second_half], store.at[1]),
-            pltpu.make_async_copy(w.at[ITERS - 1], last_w.at[:, first_half], store.at[2]),
-            pltpu.make_async_copy(wba, last_w.at[:, second_half], store.at[3]),
-        ]
-
-        @pl.when(it == ITERS - 1)
-        def _():
-            stores[0].start()
-            stores[1].start()
-
+            cab[...] = dot(waa[it], gab, ((1,), (0,)), HIGHEST)
+            m[...] = gbb - dot(cab[...], cab[...], ((0,), (0,)), HIGHEST)
+
+            @pl.when(it == 0)
+            def _():
+                arrived(edges())
+                for copy in passes((me, 0)):
+                    copy.wait_recv()
+
+        shift = dot(waa[it], cab[...], ((0,), (0,)), HIGHEST)
+        rest[...] = y3[it] - dot(other[it], shift, ((1,), (0,)), HIGHEST)
         for g, group in enumerate(inverse_factor([m[8 * i : 8 * i + 8, :] for i in range(16)])):
             w[it, 8 * g : 8 * g + 8, :] = group
 
-        pl.when(it == ITERS - 1)(stores[2].start)
-
-        def update(new_rows, arrive):
-            @pl.when(it == 0)
-            def _():
-                x[...] = new_rows(own)
-                z[DEGREE, own, :] = x[...].astype(BF16)
-                arrive()
-                for rows in (slice(0, LOW), slice(LOW + OWN, EXT)):
-                    z[DEGREE, rows, :] = new_rows(rows).astype(BF16)
+        pl.when(core == 0)(give_w.start)
+
+        @pl.when(it == ITERS - 1)
+        def _():
+            stores = [
+                pltpu.make_async_copy(rest.at[pl.ds(LOW, OWN)], last_y, store.at[0]),
+                pltpu.make_async_copy(w.at[ITERS - 1], last_w, store.at[1]),
+            ]
+            for copy in stores:
+                copy.start()
+            for copy in stores:
+                copy.wait()
+
+        @pl.when(it == 0)
+        def _():
+            new = dot(rest[...], w[it], ((1,), (1,)), HIGHEST)
+            x[...] = new[own, :]
+            z[DEGREE] = new.astype(BF16)
 
         @pl.when(core == 0)
         def _():
-            give_w.start()
-            update(lambda rows: dot(y3[it, rows, :], w[it], ((1,), (1,)), HIGHEST), lambda: None)
             give_y.wait_send()
             give_w.wait_send()
 
@@ -332,27 +343,6 @@
             def _():
                 for copy in passes((me, 1)):
                     copy.wait_send()
-
-        @pl.when(core == 1)
-        def _():
-            wba[...] = -dot(w[it], shift[...], ((1,), (1,)), HIGHEST)
-
-            def new_rows(rows):
-                both = jnp.concatenate([y3[it, rows, :], other[it, rows, :]], axis=1)
-                return dot(both, jnp.concatenate([w[it], wba[...]], axis=1), ((1,), (1,)), HIGHEST)
-
-            def arrive():
-                arrived(edges())
-                for copy in passes((me, 0)):
-                    copy.wait_recv()
-
-            update(new_rows, arrive)
-
-        @pl.when(it == ITERS - 1)
-        def _():
-            stores[3].start()
-            for copy in stores:
-                copy.wait()
 
         @pl.when(it == 0)
         def _():
@@ -378,21 +368,22 @@
 
     last_y, last_w = pl.pallas_call(
         functools.partial(kernel, axes),
-        out_shape=(jax.ShapeDtypeStruct((OWN, 2 * TILE), F32), jax.ShapeDtypeStruct((TILE, 2 * TILE), F32)),
-        in_specs=[pl.BlockSpec(memory_space=pltpu.SMEM), ANY, ANY],
+        out_shape=(jax.ShapeDtypeStruct((OWN, TILE), F32), jax.ShapeDtypeStruct((TILE, TILE), F32)),
+        in_specs=[ANY, ANY, ANY],
         out_specs=(ANY, ANY),
         scratch_shapes=[
+            pltpu.SMEM((BR * TPR,), jnp.int32),
             vmem(BR * TPR, TILE, TILE, dtype=BF16),
             vmem(2, OWN, EXT, dtype=BF16),
             vmem(OWN, TILE),
             vmem(steps, EXT, TILE, dtype=BF16),
             vmem(OWN, TILE), vmem(OWN, TILE), vmem(ITERS, EXT, TILE), vmem(ITERS, EXT, TILE),
-            vmem(TILE, TILE), vmem(ITERS, TILE, TILE), vmem(ITERS, TILE, TILE), vmem(TILE, TILE), vmem(TILE, TILE),
+            vmem(TILE, TILE), vmem(ITERS, TILE, TILE), vmem(ITERS, TILE, TILE), vmem(TILE, TILE), vmem(EXT, TILE),
             vmem(ITERS, NQ, rows_a, TILE), vmem(ITERS, NQ, rows_b, TILE),
             vmem(ITERS, NQ, rows_a, TILE), vmem(ITERS, NQ, rows_b, TILE),
             vmem(ITERS, NZ, rows_a, TILE), vmem(ITERS, NZ, rows_b, TILE),
             vmem(ITERS, NQ, rows_a, TILE), vmem(ITERS, NQ, rows_b, TILE),
-            dma((2,)), dma((4,)), dma((steps, 2)), dma((steps, 2)), dma((ITERS, 2)), dma((ITERS, 2)),
+            dma((3,)), dma((2,)), dma((steps, 2)), dma((steps, 2)), dma((ITERS, 2)), dma((ITERS, 2)),
             dma((2,)), dma((2,)), dma((2,)), dma((2,)),
         ] + [dma((ITERS,))] * 6,
         compiler_params=pltpu.CompilerParams(collective_id=0, has_side_effects=True),

time: 105 us -> 104 us (level)
  no operation moved by 1% of the time
where the time goes in v5:
time: 104 us
  Pallas kernels  102 us (98%)
  matrix products  1.94 us (2%)
    pallas_call x1, Pallas kernels, per_device(): pl.pallas_call(functools.partial(kernel, axes), out_shape=(jax.ShapeDtype...  102 us

profile of v5, /device:TPU:1, one launch (start us, length us, event | category | flops | bytes accessed | tf_op | source)
XLA Modules:
  0.0 104.2 jit_solution(4692794728163544345)
XLA Ops:
  0.0 102.2 %embed.1 = (f32[384,128]{1,0:T(8,128)}, f32[128,128]{1,0:T(8,128)}) custom-call(s32[36]{0:T(128)} %cols_hbm.1, f32[384,128]{1,0:T(8,128)} %x_ref.1, bf16[36,128,128]{2,1,0:T(8,128)(2,1)} %tiles_ref.1), custom_call_target="tpu_custom_call" | custom-call | tf_op jit(solution)/shard_map/embed/pallas_call | solution.py:369
  102.2 1.9 %fusion = f32[384,128]{1,0:T(8,128)} fusion(f32[384,128]{1,0:T(8,128)} %get-tuple-element.7, f32[128,128]{1,0:T(8,128)} %get-tuple-element.8), kind=kOutput, calls=%fused_computation | convolution fusion | flops 75497472 | bytes 458752 | tf_op jit(solution)/shard_map/dot_general | solution.py:29

commit v6 on v5

--- a/solution.py
+++ b/solution.py
@@ -369,7 +369,7 @@
     last_y, last_w = pl.pallas_call(
         functools.partial(kernel, axes),
         out_shape=(jax.ShapeDtypeStruct((OWN, TILE), F32), jax.ShapeDtypeStruct((TILE, TILE), F32)),
-        in_specs=[ANY, ANY, ANY],
+        in_specs=[pl.BlockSpec(memory_space=pltpu.HBM)] * 3,
         out_specs=(ANY, ANY),
         scratch_shapes=[
             pltpu.SMEM((BR * TPR,), jnp.int32),
@@ -386,9 +386,11 @@
             dma((3,)), dma((2,)), dma((steps, 2)), dma((steps, 2)), dma((ITERS, 2)), dma((ITERS, 2)),
             dma((2,)), dma((2,)), dma((2,)), dma((2,)),
         ] + [dma((ITERS,))] * 6,
-        compiler_params=pltpu.CompilerParams(collective_id=0, has_side_effects=True),
+        compiler_params=pltpu.CompilerParams(
+            collective_id=0, has_side_effects=True, vmem_limit_bytes=24 * 2**20
+        ),
         name="embed",
-    )(tile_cols, start, tiles)
+    )(*[pltpu.with_memory_space_constraint(a, pltpu.HBM) for a in (tile_cols, start, tiles)])
     return dot(last_y, last_w, ((1,), (1,)), HIGHEST)
 
 

time: 104 us -> 103 us (level)
  no operation moved by 1% of the time
where the time goes in v6:
time: 103 us
  Pallas kernels  102 us (99%)
    pallas_call x1, Pallas kernels, per_device(): pl.pallas_call(functools.partial(kernel, axes), out_shape=(jax.ShapeDtype...  102 us

profile of v6, /device:TPU:1, one launch (start us, length us, event | category | flops | bytes accessed | tf_op | source)
XLA Modules:
  0.0 103.0 jit_solution(5022204858875970550)
XLA Ops:
  0.0 102.0 %embed.1 = (f32[384,128]{1,0:T(8,128)S(1)}, f32[128,128]{1,0:T(8,128)S(1)}) custom-call(s32[36]{0:T(128)} %cols_hbm.1, f32[384,128]{1,0:T(8,128)} %x_ref.1, bf16[36,128,128]{2,1,0:T(8,128)(2,1)} %tiles_ref.1), custom_call_target="tpu_custom_call" | custom-call | tf_op jit(solution)/shard_map/embed/pallas_call | solution.py:369
  102.0 1.0 fusion

commit v7 on v6

--- a/solution.py
+++ b/solution.py
@@ -182,8 +182,8 @@
         down, up = halo(s)
         product = band_dot(slice(LOW, LOW + OWN), z[s, LOW : LOW + OWN, :])
         pl.when(jnp.logical_and(travelled, has_left))(up.wait_recv)
+        pl.when(jnp.logical_and(travelled, has_right))(down.wait_recv)
         product += band_dot(slice(0, LOW), z[s, 0:LOW, :])
-        pl.when(jnp.logical_and(travelled, has_right))(down.wait_recv)
         product += band_dot(slice(LOW + OWN, EXT), z[s, LOW + OWN : EXT, :])
         return product
 

time: 103 us -> 103 us (level)
  no operation moved by 1% of the time
where the time goes in v7:
time: 103 us
  Pallas kernels  102 us (99%)
    pallas_call x1, Pallas kernels, per_device(): pl.pallas_call(functools.partial(kernel, axes), out_shape=(jax.ShapeDtype...  102 us

profile of v7, /device:TPU:1, one launch (start us, length us, event | category | flops | bytes accessed | tf_op | source)
XLA Modules:
  0.0 103.0 jit_solution(7860075168005851155)
XLA Ops:
  0.0 102.0 %embed.1 = (f32[384,128]{1,0:T(8,128)S(1)}, f32[128,128]{1,0:T(8,128)S(1)}) custom-call(s32[36]{0:T(128)} %cols_hbm.1, f32[384,128]{1,0:T(8,128)} %x_ref.1, bf16[36,128,128]{2,1,0:T(8,128)(2,1)} %tiles_ref.1), custom_call_target="tpu_custom_call" | custom-call | tf_op jit(solution)/shard_map/embed/pallas_call | solution.py:369
  102.0 1.0 fusion

commit v8 on v7

--- a/solution.py
+++ b/solution.py
@@ -174,9 +174,8 @@
         pl.when(has_left)(pair[1].wait_recv)
 
     def band_dot(lanes, values):
-        return dot(band[0, :, lanes], values, ((1,), (0,))) + dot(
-            band[1, :, lanes], values, ((1,), (0,))
-        )
+        both = dot(band[:, :, lanes].reshape(2 * OWN, values.shape[0]), values, ((1,), (0,)))
+        return both[:OWN] + both[OWN:]
 
     def apply(s, travelled=True):
         down, up = halo(s)

time: 103 us -> 103 us (level)
  no operation moved by 1% of the time
where the time goes in v8:
time: 103 us
  Pallas kernels  102 us (99%)
    pallas_call x1, Pallas kernels, per_device(): pl.pallas_call(functools.partial(kernel, axes), out_shape=(jax.ShapeDtype...  102 us

profile of v8, /device:TPU:1, one launch (start us, length us, event | category | flops | bytes accessed | tf_op | source)
XLA Modules:
  0.0 103.1 jit_solution(9353270890682701672)
XLA Ops:
  0.0 102.1 %embed.1 = (f32[384,128]{1,0:T(8,128)S(1)}, f32[128,128]{1,0:T(8,128)S(1)}) custom-call(s32[36]{0:T(128)} %cols_hbm.1, f32[384,128]{1,0:T(8,128)} %x_ref.1, bf16[36,128,128]{2,1,0:T(8,128)(2,1)} %tiles_ref.1), custom_call_target="tpu_custom_call" | custom-call | tf_op jit(solution)/shard_map/embed/pallas_call | solution.py:368
  102.1 1.0 fusion
